TPU v7x, 512 devices: a whole 4x8x8 slice. The times are simulated.
512 devices in a mesh: seq: 128 (over z, y, core), tp: 4 (over x).
Axes of the slice: x: 4, y: 8, z: 8, core: 2. Of those that a mesh axis runs over, the one named last changes fastest.
Arguments:
- queries: bfloat16 [32768, 4096], P('seq', 'tp'), may hold values from -6 to 6, as said below
- keys: bfloat16 [32768, 512], P('seq', 'tp'), may hold values from -6 to 6, as said below
- values: bfloat16 [32768, 512], P('seq', 'tp'), may hold values from -6 to 6
- segment: int32 [32768], P('seq'), may hold values from 0 to 255, never falling along the last dimension, each value on 1 to 512 neighbouring positions
- repack: int32 [32768], P('seq'), may hold values from 0 to 32767, as said below
- proj: bfloat16 [1536, 4096], P('seq', 'tp'), may hold values from -0.5 to 0.5
- student_states: bfloat16 [32768, 1536], P('seq'), may hold values from -6 to 6
- target_row: int32 [32768], P('seq'), may hold values from 0 to 255
Outputs:
- student_rows: bfloat16 [32768, 1536], P('seq', 'tp')
- grad: float32 [1536, 4096], P('seq', 'tp')
Inputs may be any that keep to these rules, and one draw needn't show every extreme that they name: `queries`: scaled normal entries. `keys`: scaled normal entries. `repack`: A permutation of the student rows. Each device's teacher rows go in consecutive groups of 4 rows, in order, each group to one student owner (the device holding student rows owner * 256 to owner * 256 + 255); every device sends exactly 4 rows to each of 64 other devices and none to itself, so at most 4 rows from one device to one owner, reached by every sending pair.
All inputs are finite; a program needn't handle non-finite values.
Results may differ from a plain program's by a relative error of at most 0.0056.
Values may be sent and summed in bfloat16 or wider, within the bound.
No kernel may reach another device: no remote copies, remote signals or barrier semaphores. Data moves between devices by JAX's collectives and lax.ppermute only.
A program may use at most 64 MiB of HBM per device.

v0:
```python
import math
import jax
import jax.numpy as jnp
from jax import lax
from jax.sharding import PartitionSpec as P

HEADS = 32
KV_HEADS = 4
HEAD_DIM = 128
SW = 1536
REACH = 2
GROUP_ROWS = 4
neg_large = -1e30


def passed_along(block, axis, distance):
    devices = range(lax.axis_size(axis))
    route = [(i - distance, i) for i in devices if i - distance in devices]
    return lax.ppermute(block, axis, route)


def attend(queries, keys, values, segment):
    row_count = queries.shape[0]
    lanes = keys.shape[1]
    seg_rows = (segment + 1).astype(jnp.bfloat16).reshape(-1, lanes)
    seg_rows = jnp.concatenate([seg_rows, jnp.zeros((14, lanes), jnp.bfloat16)], 0)
    packed = jnp.concatenate([keys, values, seg_rows], 0)
    blocks = [packed]
    for step in range(1, REACH + 1):
        blocks.insert(0, passed_along(packed, "seq", step))
    all_keys = jnp.concatenate([b[:row_count] for b in blocks], 0)
    all_values = jnp.concatenate([b[row_count : 2 * row_count] for b in blocks], 0)
    key_seg = jnp.concatenate(
        [b[2 * row_count : 2 * row_count + 2].reshape(-1) for b in blocks], 0
    ).astype(jnp.int32)
    key_pos = jnp.arange(3 * row_count, dtype=jnp.int32) - REACH * row_count
    row_pos = jnp.arange(row_count, dtype=jnp.int32)
    allowed = (key_seg[None, :] == (segment + 1)[:, None]) & (key_pos[None, :] <= row_pos[:, None])
    group = HEADS // KV_HEADS
    q_heads = queries.reshape(row_count, group, HEAD_DIM)
    scale = 1.0 / math.sqrt(HEAD_DIM)
    outputs = []
    for head in range(group):
        scores = (
            jnp.einsum("td,sd->ts", q_heads[:, head], all_keys, preferred_element_type=jnp.float32)
            * scale
        )
        scores = jnp.where(allowed, scores, neg_large)
        top = jnp.max(scores, axis=-1, keepdims=True)
        expo = jnp.exp(scores - top)
        weights = (expo / jnp.sum(expo, axis=-1, keepdims=True)).astype(jnp.bfloat16)
        mixed = jnp.einsum("ts,sd->td", weights, all_values, preferred_element_type=jnp.float32)
        outputs.append(mixed.astype(jnp.bfloat16))
    return jnp.concatenate(outputs, axis=1)


def on_device(queries, keys, values, segment, repack, proj, student_states, target_row):
    row_count = queries.shape[0]
    devices = lax.axis_size("seq")
    groups = row_count // GROUP_ROWS
    attended = attend(queries, keys, values, segment)
    target_dev = repack // row_count
    local_slot = repack - target_dev * row_count
    owners = target_dev.reshape(groups, GROUP_ROWS)[:, 0]
    owner_hot = owners[None, :] == jnp.arange(devices, dtype=jnp.int32)[:, None]
    slots_by_group = local_slot.reshape(groups, GROUP_ROWS)
    slot_table = jnp.sum(jnp.where(owner_hot[:, :, None], slots_by_group[None], 0), axis=1)
    slot_table = jnp.where(jnp.any(owner_hot, axis=1)[:, None], slot_table, row_count)
    slots = lax.all_to_all(slot_table, "seq", split_axis=0, concat_axis=0, tiled=True)
    width_share = SW // lax.axis_size("tp")
    tp_index = lax.axis_index("tp")
    targets = student_states[target_row]
    bucket_dev = jnp.arange(devices * GROUP_ROWS, dtype=jnp.int32) // GROUP_ROWS
    bucket_pos = jnp.arange(devices * GROUP_ROWS, dtype=jnp.int32) % GROUP_ROWS
    row_ids = jnp.arange(row_count, dtype=jnp.int32)
    pick = (
        (bucket_dev[:, None] == target_dev[None, :])
        & (bucket_pos[:, None] == (row_ids % GROUP_ROWS)[None, :])
    ).astype(jnp.bfloat16)
    buckets = jnp.dot(pick, attended, preferred_element_type=jnp.float32).astype(jnp.bfloat16)
    arrived = lax.all_to_all(buckets, "seq", split_axis=0, concat_axis=0, tiled=True)
    place = (row_ids[:, None] == slots.reshape(-1)[None, :]).astype(jnp.bfloat16)
    student_x = jnp.dot(place, arrived, preferred_element_type=jnp.float32).astype(jnp.bfloat16)
    all_proj = lax.all_gather(proj, "seq", axis=0, tiled=True)
    y_part = jnp.einsum("tf,nf->tn", student_x, all_proj, preferred_element_type=jnp.float32)
    y_total = lax.psum(y_part, "tp")
    y_rounded = y_total.astype(jnp.bfloat16)
    delta = (y_rounded.astype(jnp.float32) - targets.astype(jnp.float32)).astype(jnp.bfloat16)
    out_rows = lax.dynamic_slice_in_dim(y_rounded, tp_index * width_share, width_share, 1)
    norm_factor = 1.0 / math.sqrt(row_count * devices)
    grad_rows = delta.shape[1] // devices
    term = jnp.einsum("ts,tf->sf", delta, student_x, preferred_element_type=jnp.float32)
    pieces = term.reshape(devices, grad_rows, term.shape[1])
    summed = lax.all_to_all(
        pieces.astype(jnp.bfloat16), "seq", split_axis=0, concat_axis=0, tiled=True
    ).astype(pieces.dtype)
    grad = jnp.sum(summed, axis=0) * norm_factor
    return (out_rows, grad)


def solution(mesh):
    placed = (
        P("seq", "tp"),
        P("seq", "tp"),
        P("seq", "tp"),
        P("seq"),
        P("seq"),
        P("seq", "tp"),
        P("seq", None),
        P("seq"),
    )
    return jax.shard_map(
        on_device,
        mesh=mesh,
        in_specs=placed,
        out_specs=(P("seq", "tp"), P("seq", "tp")),
        check_vma=False,
    )
```

profile of v0, /device:TPU:41, one launch (start us, length us, event | category | flops | bytes accessed | tf_op | source)
XLA Modules:
  0.0 316.8 jit_solution(7449039841433495899)
XLA Ops:
  7.2 0.0 copy-start
  7.2 0.0 copy-start.1
  7.2 0.8 broadcast_add_fusion
  8.0 0.1 pad.12.clone
  8.0 1.0 maximum_maximum_fusion
  9.1 2.9 collective-permute-start.1
  11.9 2.3 collective-permute-start
  14.2 0.7 multiply_subtract_fusion
  14.9 0.1 broadcast_in_dim.51
  15.1 0.1 copy.28
  15.1 0.1 reshape.146
  15.2 0.1 slice_reduce_fusion
  15.4 0.1 fusion.48
  15.5 0.1 select_reduce_fusion
  15.6 0.7 copy.29
  16.3 16.6 %all-to-all-start = ((s32[128,1,4]{2,1,0:T(1,128)}), s32[128,1,4]{2,1,0:T(1,128)S(1)}, u32[]{:S(2)}, u32[]{:S(2)}) async-start(s32[128,1,4]{2,1,0:T(1,128)} %copy.29), calls=%async_computation | async-start | bytes 131072 | tf_op jit(solution)/shard_map/all_to_all | solution.py:69
  33.0 0.0 all-gather.3.cloned.1.call-start
  33.0 0.7 all-gather.3.cloned.1.call-update
  33.7 1.2 copy.30
  35.1 1.2 fusion.52
  36.3 0.3 fusion.53
  36.6 0.3 fusion.54
  37.0 0.4 fusion.55
  37.3 0.2 fusion.25
  37.5 0.2 fusion.26
  37.7 0.2 fusion.27
  37.8 0.2 fusion.28
  38.0 0.3 fusion.56
  38.4 0.2 fusion.29
  38.5 0.4 fusion.57
  38.9 0.2 fusion.30
  39.1 0.3 fusion.58
  39.4 0.2 fusion.31
  39.6 0.3 fusion.59
  40.0 0.2 fusion.32
  40.1 0.3 fusion.16
  40.4 0.3 fusion.17
  40.7 0.3 fusion.18
  41.0 0.3 fusion.19
  41.3 0.3 fusion.20
  41.6 0.3 fusion.21
  41.9 0.3 fusion.22
  42.2 0.3 fusion.23
  42.6 0.5 convolution_convert_fusion.1
  43.0 1.2 all_to_all.16
  44.3 13.7 %all-to-all-start.1 = ((bf16[128,4,1024]{2,1,0:T(4,128)(2,1)}), bf16[128,4,1024]{2,1,0:T(4,128)(2,1)S(1)}, u32[]{:S(2)}, u32[]{:S(2)}) async-start(bf16[128,4,1024]{2,1,0:T(4,128)(2,1)} %all_to_all.16), calls=%async_computation.1 | async-start | bytes 2097152 | tf_op jit(solution)/shard_map/all_to_all | solution.py:81
  58.1 1.3 gather_fusion
  59.4 0.5 broadcast.182
  59.9 0.8 reduce.5
  60.7 0.1 eq.82
  60.8 26.4 %all-to-all-done.1 = bf16[128,4,1024]{2,1,0:T(4,128)(2,1)S(1)} async-done(((bf16[128,4,1024]{2,1,0:T(4,128)(2,1)}), bf16[128,4,1024]{2,1,0:T(4,128)(2,1)S(1)}, u32[]{:S(2)}, u32[]{:S(2)}) %all-to-all-start.1) | async-done | bytes 1048608 | tf_op jit(solution)/shard_map/all_to_all | solution.py:81
  87.2 1.1 all_to_all.18
  88.3 1.7 convolution_convert_fusion.2
  90.0 46.0 %all-gather.3.cloned.1.call-done = bf16[128,12,1024]{2,1,0:T(8,128)(2,1)} async-done(((bf16[1,12,1024]{2,1,0:T(8,128)(2,1)}), bf16[128,12,1024]{2,1,0:T(8,128)(2,1)}) %all-gather.3.cloned.1.call-update) | async-done | bytes 3145744 | tf_op jit(solution)/shard_map/all_gather | solution.py:84
  136.0 6.2 %reshape.159 = bf16[1536,1024]{1,0:T(8,128)(2,1)} reshape(bf16[128,12,1024]{2,1,0:T(8,128)(2,1)} %all-gather.3.cloned.1.call-done) | data formatting | bytes 6291456
  142.2 4.1 %fusion.60 = f32[256,1536]{1,0:T(8,128)} fusion(bf16[256,1024]{1,0:T(8,128)(2,1)S(1)} %convolution_convert_fusion.2, bf16[1536,1024]{1,0:T(8,128)(2,1)} %reshape.159), kind=kOutput, calls=%fused_computation.134 | convolution fusion | flops 805306368 | bytes 5242880 | tf_op jit(solution)/shard_map/tf,nf->tn/dot_general | solution.py:85
  146.2 33.8 %all-reduce.1 = bf16[256,1536]{1,0:T(8,128)(2,1)S(1)} all-reduce(f32[256,1536]{1,0:T(8,128)} %fusion.60), channel_id=1, replica_groups=mesh['seq'=128,'tp'=4] {'tp'}, use_global_device_ids=true, to_apply=%region_18.19 | all-reduce | flops 393216 | bytes 2359296 | tf_op jit(solution)/shard_map/psum | solution.py:86
  180.0 2.7 convolution_convert_fusion
  182.7 6.1 %convert_element_type.112 = bf16[128,12,1024]{2,1,0:T(8,128)(2,1)} reshape(bf16[1536,1024]{1,0:T(8,128)(2,1)} %convolution_convert_fusion) | data formatting | bytes 6291456 | tf_op jit(solution)/shard_map/convert_element_type | solution.py:95
  188.8 13.8 %all-to-all-start.2 = ((bf16[128,12,1024]{2,1,0:T(8,128)(2,1)}), bf16[128,12,1024]{2,1,0:T(8,128)(2,1)}, u32[]{:S(2)}, u32[]{:S(2)}) async-start(bf16[128,12,1024]{2,1,0:T(8,128)(2,1)} %convert_element_type.112), calls=%async_computation.2 | async-start | bytes 8388608 | tf_op jit(solution)/shard_map/all_to_all | solution.py:94
  202.6 0.7 constant_dynamic-slice_fusion
  203.3 103.0 %all-to-all-done.2 = bf16[128,12,1024]{2,1,0:T(8,128)(2,1)} async-done(((bf16[128,12,1024]{2,1,0:T(8,128)(2,1)}), bf16[128,12,1024]{2,1,0:T(8,128)(2,1)}, u32[]{:S(2)}, u32[]{:S(2)}) %all-to-all-start.2) | async-done | bytes 3145760 | tf_op jit(solution)/shard_map/all_to_all | solution.py:94
  306.3 3.0 convert_reduce_fusion
  309.3 0.6 broadcast_multiply_fusion
  (21 shorter events, 0.1 us)
Async XLA Ops:
  7.2 50.9 %copy-start = (bf16[256,1536]{1,0:T(8,128)(2,1)S(1)}, bf16[256,1536]{1,0:T(8,128)(2,1)}, u32[]{:S(2)}) copy-start(bf16[256,1536]{1,0:T(8,128)(2,1)} %param.14) | copy-start | bytes 2359300
  7.2 29.1 %copy-start.1 = (bf16[256,128]{1,0:T(8,128)(2,1)S(1)}, bf16[256,128]{1,0:T(8,128)(2,1)}, u32[]{:S(2)}) copy-start(bf16[256,128]{1,0:T(8,128)(2,1)} %param.9) | copy-start | bytes 196612
  9.1 25.9 %collective-permute-start.1 = (bf16[528,128]{1,0:T(8,128)(2,1)S(1)}, bf16[528,128]{1,0:T(8,128)(2,1)S(1)}, u32[]{:S(2)}, u32[]{:S(2)}) collective-permute-start(bf16[528,128]{1,0:T(8,128)(2,1)S(1)} %maximum_maximum_fusion), channel_id=1, source_target_pairs={{0,4},{4,8},{8,12},{12,16},{16,20},{20,24},{24,28},{28,32},{32,36}... | collective-permute-start | bytes 405512 | tf_op jit(solution)/shard_map/ppermute | solution.py:19
  11.9 23.1 %collective-permute-start = (bf16[528,128]{1,0:T(8,128)(2,1)S(1)}, bf16[528,128]{1,0:T(8,128)(2,1)S(1)}, u32[]{:S(2)}, u32[]{:S(2)}) collective-permute-start(bf16[528,128]{1,0:T(8,128)(2,1)S(1)} %maximum_maximum_fusion), channel_id=1, source_target_pairs={{0,8},{4,12},{8,16},{12,20},{16,24},{20,28},{24,32},{28,36},{32,40... | collective-permute-start | bytes 405512 | tf_op jit(solution)/shard_map/ppermute | solution.py:19
  16.3 28.0 %all-to-all-start = ((s32[128,1,4]{2,1,0:T(1,128)}), s32[128,1,4]{2,1,0:T(1,128)S(1)}, u32[]{:S(2)}, u32[]{:S(2)}) async-start(s32[128,1,4]{2,1,0:T(1,128)} %copy.29), calls=%async_computation | async-start | bytes 131072 | tf_op jit(solution)/shard_map/all_to_all | solution.py:69
  33.0 103.0 %all-gather.3.cloned.1.call-start = ((), (), s32[]{:S(2)}) async-start(), calls=%async_computation.3 | async-start | bytes 4227072 | tf_op jit(solution)/shard_map/all_gather | solution.py:84
  38.9 1.2 copy-start.2
  42.5 15.5 %copy-start.3 = (s32[256]{0:T(256)S(1)}, s32[256]{0:T(256)}, u32[]{:S(2)}) copy-start(s32[256]{0:T(256)} %param.15) | copy-start | bytes 3076
  44.3 42.9 %all-to-all-start.1 = ((bf16[128,4,1024]{2,1,0:T(4,128)(2,1)}), bf16[128,4,1024]{2,1,0:T(4,128)(2,1)S(1)}, u32[]{:S(2)}, u32[]{:S(2)}) async-start(bf16[128,4,1024]{2,1,0:T(4,128)(2,1)} %all_to_all.16), calls=%async_computation.1 | async-start | bytes 2097152 | tf_op jit(solution)/shard_map/all_to_all | solution.py:81
  188.8 117.5 %all-to-all-start.2 = ((bf16[128,12,1024]{2,1,0:T(8,128)(2,1)}), bf16[128,12,1024]{2,1,0:T(8,128)(2,1)}, u32[]{:S(2)}, u32[]{:S(2)}) async-start(bf16[128,12,1024]{2,1,0:T(8,128)(2,1)} %convert_element_type.112), calls=%async_computation.2 | async-start | bytes 8388608 | tf_op jit(solution)/shard_map/all_to_all | solution.py:94
Sparse Core Ops, SparseCore 0:
  36.9 99.0 all-gather.2
where the time goes:
time: 318 us; the launch traced here: 317 us
  waiting for transfers between devices  176 us (55%)
  starting transfers between devices  49.4 us (16%)
  blocking collectives  33.8 us (11%)
  local copies, waits for them, and re-layouts  19.7 us (6%)
  matrix products  14.9 us (5%)
  between operations  14.4 us (5%)
  other arithmetic  8.56 us (3%)
    all_to_all x1, waiting for transfers between devices, on_device(): lax.all_to_all(pieces.astype(jnp.bfloat16), 'seq', split_axis=0, concat_a...  103 us
    all_gather x1, waiting for transfers between devices, on_device(): all_proj = lax.all_gather(proj, 'seq', axis=0, tiled=True)  46 us
    psum x1, blocking collectives, on_device(): y_total = lax.psum(y_part, 'tp')  33.8 us
    all_to_all x1, waiting for transfers between devices, on_device(): lax.all_to_all(buckets, 'seq', split_axis=0, concat_axis=0, tiled=True)  26.4 us
    all_to_all x1, starting transfers between devices, on_device(): lax.all_to_all(slot_table, 'seq', split_axis=0, concat_axis=0, tiled=True)  16.6 us
    all_to_all x1, starting transfers between devices, on_device(): lax.all_to_all(pieces.astype(jnp.bfloat16), 'seq', split_axis=0, concat_a...  13.8 us
    all_to_all x1, starting transfers between devices, on_device(): lax.all_to_all(buckets, 'seq', split_axis=0, concat_axis=0, tiled=True)  13.7 us
    unnamed x10, local copies, waits for them, and re-layouts  7.43 us
  transfers between devices with their start and end apart: 6, of which 3 were waited for; matrix products, arithmetic and copies ran while one was open for 5% of the time, Pallas kernels for 0%

commit v1 on v0

--- a/solution.py
+++ b/solution.py
@@ -81,7 +81,9 @@
     arrived = lax.all_to_all(buckets, "seq", split_axis=0, concat_axis=0, tiled=True)
     place = (row_ids[:, None] == slots.reshape(-1)[None, :]).astype(jnp.bfloat16)
     student_x = jnp.dot(place, arrived, preferred_element_type=jnp.float32).astype(jnp.bfloat16)
-    all_proj = lax.all_gather(proj, "seq", axis=0, tiled=True)
+    all_proj = jnp.concatenate(
+        lax.all_to_all(jnp.stack([proj] * lax.axis_size("seq")), "seq", 0, 0), axis=0
+    )
     y_part = jnp.einsum("tf,nf->tn", student_x, all_proj, preferred_element_type=jnp.float32)
     y_total = lax.psum(y_part, "tp")
     y_rounded = y_total.astype(jnp.bfloat16)

time: 318 us -> 369 us (1.16)
  blocking collectives: 33.8 us -> 75.9 us
  waiting for transfers between devices: 176 us -> 198 us
  between operations: 14.4 us -> 0.97 us
    all_to_all x1, waiting for transfers between devices: 26.4 us -> 95.4 us  [on_device(): lax.all_to_all(jnp.stack([proj] * lax.axis_size('seq')), 'seq', 0, 0)]
    all_gather x1 -> x0, waiting for transfers between devices: 46 us -> none  [on_device(): all_proj = lax.all_gather(proj, 'seq', axis=0, tiled=True)]
    all_to_all x0 -> x1, blocking collectives: none -> 42.3 us  [on_device(): lax.all_to_all(buckets, 'seq', split_axis=0, concat_axis=0, tiled=True)]
    reshape x0 -> x1, local copies, waits for them, and re-layouts: none -> 6.16 us  [on_device(): jnp.concatenate(lax.all_to_all(jnp.stack([proj] * lax.axis_size('seq')),...]
    unnamed x10 -> x11, local copies, waits for them, and re-layouts: 7.43 us -> 1.28 us
    all_to_all x1, starting transfers between devices: 13.7 us -> 9.14 us  [on_device(): lax.all_to_all(jnp.stack([proj] * lax.axis_size('seq')), 'seq', 0, 0)]
  transfers between devices with their start and end apart: 6 -> 5, of which waited for: 3 -> 2; matrix products, arithmetic and copies ran while one was open for 5% -> 4% of each run, Pallas kernels for 0% -> 0%
where the time goes in v1:
time: 369 us; the launch traced here: 368 us
  waiting for transfers between devices  198 us (54%)
  blocking collectives  75.9 us (21%)
  starting transfers between devices  47.3 us (13%)
  local copies, waits for them, and re-layouts  21.5 us (6%)
  matrix products  14.9 us (4%)
  other arithmetic  8.56 us (2%)
    all_to_all x1, waiting for transfers between devices, on_device(): lax.all_to_all(pieces.astype(jnp.bfloat16), 'seq', split_axis=0, concat_a...  103 us
    all_to_all x1, waiting for transfers between devices, on_device(): lax.all_to_all(jnp.stack([proj] * lax.axis_size('seq')), 'seq', 0, 0)  95.4 us
    all_to_all x1, blocking collectives, on_device(): lax.all_to_all(buckets, 'seq', split_axis=0, concat_axis=0, tiled=True)  42.3 us
    psum x1, blocking collectives, on_device(): y_total = lax.psum(y_part, 'tp')  33.6 us
    all_to_all x1, starting transfers between devices, on_device(): lax.all_to_all(slot_table, 'seq', split_axis=0, concat_axis=0, tiled=True)  16.6 us
    all_to_all x1, starting transfers between devices, on_device(): lax.all_to_all(pieces.astype(jnp.bfloat16), 'seq', split_axis=0, concat_a...  16.4 us
    all_to_all x1, starting transfers between devices, on_device(): lax.all_to_all(jnp.stack([proj] * lax.axis_size('seq')), 'seq', 0, 0)  9.14 us
  transfers between devices with their start and end apart: 5, of which 2 were waited for; matrix products, arithmetic and copies ran while one was open for 4% of the time, Pallas kernels for 0%

profile of v1, /device:TPU:41, one launch (start us, length us, event | category | flops | bytes accessed | tf_op | source)
XLA Modules:
  0.0 367.6 jit_solution(6320810882202520364)
XLA Ops:
  0.6 0.0 copy-start
  0.6 0.0 copy-start.1
  0.7 0.8 broadcast_add_fusion
  1.4 0.1 pad.12.clone
  1.5 1.0 maximum_maximum_fusion
  2.5 2.9 collective-permute-start.1
  5.4 2.3 collective-permute-start
  7.7 0.7 multiply_subtract_fusion
  8.4 0.1 broadcast_in_dim.51
  8.5 0.1 copy.28
  8.6 0.1 reshape.151
  8.7 0.1 slice_reduce_fusion
  8.8 0.1 fusion.48
  8.9 0.1 select_reduce_fusion
  9.0 0.7 copy.29
  9.8 16.6 %all-to-all-start = ((s32[128,1,4]{2,1,0:T(1,128)}), s32[128,1,4]{2,1,0:T(1,128)S(1)}, u32[]{:S(2)}, u32[]{:S(2)}) async-start(s32[128,1,4]{2,1,0:T(1,128)} %copy.29), calls=%async_computation | async-start | bytes 131072 | tf_op jit(solution)/shard_map/all_to_all | solution.py:69
  26.5 1.2 copy.30
  27.8 1.2 fusion.52
  29.0 0.3 fusion.53
  29.4 0.3 fusion.54
  29.7 0.3 fusion.55
  30.1 0.3 fusion.56
  30.4 0.3 fusion.57
  30.8 0.3 fusion.58
  31.1 0.3 fusion.59
  31.5 0.2 fusion.25
  31.6 0.2 fusion.26
  31.8 0.3 fusion.16
  32.1 0.3 fusion.17
  32.4 0.2 fusion.27
  32.6 0.3 fusion.18
  32.9 0.2 fusion.28
  33.1 0.3 fusion.19
  33.4 0.2 fusion.29
  33.5 0.3 fusion.20
  33.8 0.2 fusion.30
  34.0 0.3 fusion.21
  34.3 0.2 fusion.31
  34.5 0.3 fusion.22
  34.8 0.2 fusion.32
  35.0 0.3 fusion.23
  35.2 0.0 copy-start.3
  35.3 0.5 convolution_convert_fusion.1
  35.8 0.4 all_to_all.19
  36.2 42.3 %all_to_all.28 = bf16[128,4,1024]{2,1,0:T(4,128)(2,1)S(1)} all-to-all(bf16[128,4,1024]{2,1,0:T(4,128)(2,1)S(1)} %all_to_all.19), channel_id=1, replica_groups=mesh['seq'=128,'tp'=4] {'seq'}, dimensions={0} | all-to-all | bytes 2097152 | tf_op jit(solution)/shard_map/all_to_all | solution.py:81
  78.5 2.5 stack.2
  81.0 9.1 %all-to-all-start.2 = ((bf16[128,12,1024]{2,1,0:T(8,128)(2,1)}), bf16[128,12,1024]{2,1,0:T(8,128)(2,1)}, u32[]{:S(2)}, u32[]{:S(2)}) async-start(bf16[128,12,1024]{2,1,0:T(8,128)(2,1)} %stack.2), calls=%async_computation.2 | async-start | bytes 8388608 | tf_op jit(solution)/shard_map/all_to_all | solution.py:85
  90.2 1.3 gather_fusion
  91.5 0.5 broadcast.184
  92.0 0.8 reduce.5
  92.8 0.1 eq.82
  92.9 1.2 all_to_all.21
  94.2 1.7 convolution_convert_fusion.2
  95.8 95.4 %all-to-all-done.2 = bf16[128,12,1024]{2,1,0:T(8,128)(2,1)} async-done(((bf16[128,12,1024]{2,1,0:T(8,128)(2,1)}), bf16[128,12,1024]{2,1,0:T(8,128)(2,1)}, u32[]{:S(2)}, u32[]{:S(2)}) %all-to-all-start.2) | async-done | bytes 3145760 | tf_op jit(solution)/shard_map/all_to_all | solution.py:85
  191.2 6.2 %reshape.154 = bf16[1536,1024]{1,0:T(8,128)(2,1)} reshape(bf16[128,12,1024]{2,1,0:T(8,128)(2,1)} %all-to-all-done.2) | data formatting | bytes 6291456 | tf_op jit(solution)/shard_map/reshape | solution.py:84
  197.4 4.1 %fusion.60 = f32[256,1536]{1,0:T(8,128)} fusion(bf16[256,1024]{1,0:T(8,128)(2,1)S(1)} %convolution_convert_fusion.2, bf16[1536,1024]{1,0:T(8,128)(2,1)} %reshape.154), kind=kOutput, calls=%fused_computation.134 | convolution fusion | flops 805306368 | bytes 5242880 | tf_op jit(solution)/shard_map/tf,nf->tn/dot_general | solution.py:87
  201.4 33.6 %all-reduce.1 = bf16[256,1536]{1,0:T(8,128)(2,1)S(1)} all-reduce(f32[256,1536]{1,0:T(8,128)} %fusion.60), channel_id=1, replica_groups=mesh['seq'=128,'tp'=4] {'tp'}, use_global_device_ids=true, to_apply=%region_18.19 | all-reduce | flops 393216 | bytes 2359296 | tf_op jit(solution)/shard_map/psum | solution.py:88
  235.1 2.7 convolution_convert_fusion
  237.8 6.1 %convert_element_type.112 = bf16[128,12,1024]{2,1,0:T(8,128)(2,1)} reshape(bf16[1536,1024]{1,0:T(8,128)(2,1)} %convolution_convert_fusion) | data formatting | bytes 6291456 | tf_op jit(solution)/shard_map/convert_element_type | solution.py:97
  243.8 16.4 %all-to-all-start.3 = ((bf16[128,12,1024]{2,1,0:T(8,128)(2,1)}), bf16[128,12,1024]{2,1,0:T(8,128)(2,1)}, u32[]{:S(2)}, u32[]{:S(2)}) async-start(bf16[128,12,1024]{2,1,0:T(8,128)(2,1)} %convert_element_type.112), calls=%async_computation.3 | async-start | bytes 8388608 | tf_op jit(solution)/shard_map/all_to_all | solution.py:96
  260.2 0.7 constant_dynamic-slice_fusion
  260.9 103.0 %all-to-all-done.3 = bf16[128,12,1024]{2,1,0:T(8,128)(2,1)} async-done(((bf16[128,12,1024]{2,1,0:T(8,128)(2,1)}), bf16[128,12,1024]{2,1,0:T(8,128)(2,1)}, u32[]{:S(2)}, u32[]{:S(2)}) %all-to-all-start.3) | async-done | bytes 3145760 | tf_op jit(solution)/shard_map/all_to_all | solution.py:96
  363.9 3.0 convert_reduce_fusion
  366.9 0.6 broadcast_multiply_fusion
  (22 shorter events, 0.1 us)
Async XLA Ops:
  0.6 89.6 %copy-start = (bf16[256,1536]{1,0:T(8,128)(2,1)S(1)}, bf16[256,1536]{1,0:T(8,128)(2,1)}, u32[]{:S(2)}) copy-start(bf16[256,1536]{1,0:T(8,128)(2,1)} %param.14) | copy-start | bytes 2359300
  0.6 28.4 %copy-start.1 = (bf16[256,128]{1,0:T(8,128)(2,1)S(1)}, bf16[256,128]{1,0:T(8,128)(2,1)}, u32[]{:S(2)}) copy-start(bf16[256,128]{1,0:T(8,128)(2,1)} %param.9) | copy-start | bytes 196612
  2.5 25.2 %collective-permute-start.1 = (bf16[528,128]{1,0:T(8,128)(2,1)S(1)}, bf16[528,128]{1,0:T(8,128)(2,1)S(1)}, u32[]{:S(2)}, u32[]{:S(2)}) collective-permute-start(bf16[528,128]{1,0:T(8,128)(2,1)S(1)} %maximum_maximum_fusion), channel_id=1, source_target_pairs={{0,4},{4,8},{8,12},{12,16},{16,20},{20,24},{24,28},{28,32},{32,36}... | collective-permute-start | bytes 405512 | tf_op jit(solution)/shard_map/ppermute | solution.py:19
  5.4 22.3 %collective-permute-start = (bf16[528,128]{1,0:T(8,128)(2,1)S(1)}, bf16[528,128]{1,0:T(8,128)(2,1)S(1)}, u32[]{:S(2)}, u32[]{:S(2)}) collective-permute-start(bf16[528,128]{1,0:T(8,128)(2,1)S(1)} %maximum_maximum_fusion), channel_id=1, source_target_pairs={{0,8},{4,12},{8,16},{12,20},{16,24},{20,28},{24,32},{28,36},{32,40... | collective-permute-start | bytes 405512 | tf_op jit(solution)/shard_map/ppermute | solution.py:19
  9.8 26.4 %all-to-all-start = ((s32[128,1,4]{2,1,0:T(1,128)}), s32[128,1,4]{2,1,0:T(1,128)S(1)}, u32[]{:S(2)}, u32[]{:S(2)}) async-start(s32[128,1,4]{2,1,0:T(1,128)} %copy.29), calls=%async_computation | async-start | bytes 131072 | tf_op jit(solution)/shard_map/all_to_all | solution.py:69
  30.8 1.1 copy-start.2
  35.2 43.3 %copy-start.3 = (bf16[12,1024]{1,0:T(8,128)(2,1)S(1)}, bf16[12,1024]{1,0:T(8,128)(2,1)}, u32[]{:S(2)}) copy-start(bf16[12,1024]{1,0:T(8,128)(2,1)} %param.13) | copy-start | bytes 73732
  81.0 9.2 %copy-start.4 = (s32[256]{0:T(256)S(1)}, s32[256]{0:T(256)}, u32[]{:S(2)}) copy-start(s32[256]{0:T(256)} %param.15) | copy-start | bytes 3076
  81.0 110.2 %all-to-all-start.2 = ((bf16[128,12,1024]{2,1,0:T(8,128)(2,1)}), bf16[128,12,1024]{2,1,0:T(8,128)(2,1)}, u32[]{:S(2)}, u32[]{:S(2)}) async-start(bf16[128,12,1024]{2,1,0:T(8,128)(2,1)} %stack.2), calls=%async_computation.2 | async-start | bytes 8388608 | tf_op jit(solution)/shard_map/all_to_all | solution.py:85
  243.8 120.1 %all-to-all-start.3 = ((bf16[128,12,1024]{2,1,0:T(8,128)(2,1)}), bf16[128,12,1024]{2,1,0:T(8,128)(2,1)}, u32[]{:S(2)}, u32[]{:S(2)}) async-start(bf16[128,12,1024]{2,1,0:T(8,128)(2,1)} %convert_element_type.112), calls=%async_computation.3 | async-start | bytes 8388608 | tf_op jit(solution)/shard_map/all_to_all | solution.py:96
